TPU v7x, 32 devices: a whole 2x2x4 slice. The times are simulated.
32 devices in a mesh: groups: 2 (over y), expert: 4 (over z), dp: 4 (over x, core).
Axes of the slice: x: 2, y: 2, z: 4, core: 2. Of those that a mesh axis runs over, the one named last changes fastest.
Arguments:
- tokens: bfloat16 [4096, 1024], P(('groups', 'expert', 'dp')), parts along dimension 0, may hold values from -6 to 6
- expert_ids: int32 [4096, 8], P(('groups', 'expert', 'dp')), parts along dimension 0, may hold values from 0 to 63, all different within a row; in each aligned block of 128 rows (0 to 127, 128 to 255, ...) at most 16 rows name the same one
- gate_values: float32 [4096, 8], P(('groups', 'expert', 'dp')), parts along dimension 0, may hold values from 0.1 to 1
- w_gate_up: bfloat16 [64, 1024, 768], P('expert', 'dp'), may hold values from -0.1875 to 0.1875
- w_down: bfloat16 [64, 384, 1024], P('expert', None, 'dp'), may hold values from -0.3125 to 0.3125
- new_slot: int32 [64], replicated, may hold values from 0 to 63, each once
- cotangent: bfloat16 [4096, 1024], P(('groups', 'expert', 'dp')), parts along dimension 0, may hold values from -6 to 6
Outputs:
- layer_out: bfloat16 [4096, 1024], P(('groups', 'expert', 'dp')), parts along dimension 0
- d_tokens: bfloat16 [4096, 1024], P(('groups', 'expert', 'dp')), parts along dimension 0
- d_gate_up: bfloat16 [128, 1024, 768], P(('groups', 'expert'), 'dp'), parts along dimension 0
- d_down: bfloat16 [128, 384, 1024], P(('groups', 'expert'), None, 'dp'), parts along dimension 0
There are 2 independent parts, one for each index of `groups`. A program takes and returns all parts, laid end to end along the dimension named above; an argument that names none is the same for every part. Nothing has to cross between parts.
Inputs may be any that keep to these rules, and one draw needn't show every extreme that they name: `expert_ids`: each row names 8 different experts; among the 128 rows of one device no expert is named by more than 16 rows, and on some devices some expert is named by exactly 16. `new_slot`: every number appears once, so each slot holds one expert; slot s belongs to index s // (64 / 4) of axis expert.
All inputs are finite; a program needn't handle non-finite values.
Results may differ from a plain program's by a relative error of at most 0.0095.
Values may be sent and summed in bfloat16 or wider, within the bound.
No kernel may reach another device: no remote copies, remote signals or barrier semaphores. Data moves between devices by JAX's collectives and lax.ppermute only.
A program may use at most 192 MiB of HBM per device.

v0:
```python
import jax
import jax.numpy as jnp
from jax import lax
from jax.sharding import PartitionSpec as P

MOST = 16


def relocate(gate_up, down, inverse):
    expert_peers = lax.axis_size("expert")
    home_slots = gate_up.shape[0]
    spread_gu = gate_up.reshape(
        home_slots, expert_peers, gate_up.shape[1] // expert_peers, gate_up.shape[2]
    )
    spread_dn = down.reshape(home_slots, expert_peers, down.shape[1] // expert_peers, down.shape[2])
    got_gu, got_dn = (
        lax.all_to_all(spread_gu, "expert", split_axis=1, concat_axis=0, tiled=True),
        lax.all_to_all(spread_dn, "expert", split_axis=1, concat_axis=0, tiled=True),
    )
    experts = home_slots * expert_peers
    slot_order = inverse.reshape(expert_peers, home_slots).T
    pick_gu = got_gu.reshape(experts, got_gu.shape[2], got_gu.shape[3])[slot_order]
    pick_dn = got_dn.reshape(experts, got_dn.shape[2], got_dn.shape[3])[slot_order]
    new_gu, new_dn = (
        lax.all_to_all(pick_gu, "expert", split_axis=1, concat_axis=1, tiled=True),
        lax.all_to_all(pick_dn, "expert", split_axis=1, concat_axis=1, tiled=True),
    )
    return (new_gu.reshape(gate_up.shape), new_dn.reshape(down.shape))


def route_cells(expert_ids, slot_map):
    experts = slot_map.shape[0]
    flat_ids = expert_ids.reshape(-1)
    matches = flat_ids[:, None] == jnp.arange(experts, dtype=jnp.int32)[None, :]
    indicator = matches.astype(jnp.int32)
    earlier = jnp.cumsum(indicator, axis=0) - indicator
    position = jnp.sum(jnp.where(matches, earlier, 0), axis=1)
    target = jnp.sum(jnp.where(matches, slot_map[None, :], 0), axis=1)
    target_cell = target * MOST + position
    entries = flat_ids.shape[0]
    source = (
        jnp.full((experts * MOST,), entries, jnp.int32)
        .at[target_cell]
        .set(jnp.arange(entries, dtype=jnp.int32))
    )
    return (target_cell, source)


def shards(tokens, expert_ids, gate_values, w_gate_up, w_down, new_slot, cotangent):
    expert_peers = lax.axis_size("expert")
    home_slots = w_gate_up.shape[0]
    model_width = tokens.shape[1]
    hidden_width = w_down.shape[1]
    top_count = expert_ids.shape[1]
    token_count = tokens.shape[0]
    inverse = jnp.argsort(new_slot)
    local_gu, local_dn = relocate(w_gate_up, w_down, inverse)
    full_gu, full_dn = (
        lax.all_gather(local_gu, "dp", axis=1, tiled=True),
        lax.all_gather(local_dn, "dp", axis=2, tiled=True),
    )
    target_cell, source = route_cells(expert_ids, new_slot)
    blank_row = jnp.zeros((1, model_width), jnp.bfloat16)
    token_row = source // top_count
    cell_gates = jnp.concatenate([gate_values.reshape(-1), jnp.zeros((1,), jnp.float32)])[source]
    outgoing = jnp.concatenate([tokens, blank_row], axis=0)[token_row]
    cot_rows = jnp.concatenate([cotangent, blank_row], axis=0)[token_row]
    scaled_cot = (cell_gates[:, None] * cot_rows.astype(jnp.float32)).astype(jnp.bfloat16)
    row_shape = (expert_peers, home_slots, MOST, model_width)
    arrived = lax.all_to_all(
        outgoing.reshape(row_shape), "expert", split_axis=0, concat_axis=0, tiled=True
    )
    gate_up = jnp.einsum("shmd,hdf->shmf", arrived, full_gu, preferred_element_type=jnp.float32)
    gate_part = gate_up[..., :hidden_width]
    up_part = gate_up[..., hidden_width:]
    sigmoid_g = jax.nn.sigmoid(gate_part)
    silu_g = gate_part * sigmoid_g
    activation = (silu_g * up_part).astype(jnp.bfloat16)
    expert_out = jnp.einsum(
        "shmf,hfd->shmd", activation, full_dn, preferred_element_type=jnp.float32
    ).astype(jnp.bfloat16)
    returned = lax.all_to_all(expert_out, "expert", split_axis=0, concat_axis=0, tiled=True)
    gathered_out = returned.reshape(-1, model_width)[target_cell].reshape(
        token_count, top_count, model_width
    )
    layer_out = jnp.sum(gate_values[:, :, None] * gathered_out.astype(jnp.float32), axis=1).astype(
        jnp.bfloat16
    )
    d_outputs = lax.all_to_all(
        scaled_cot.reshape(row_shape), "expert", split_axis=0, concat_axis=0, tiled=True
    )
    d_act = jnp.einsum("shmd,hfd->shmf", d_outputs, full_dn, preferred_element_type=jnp.float32)
    d_gate = d_act * up_part * sigmoid_g * (1.0 + gate_part * (1.0 - sigmoid_g))
    d_up = d_act * silu_g
    d_gate_up = jnp.concatenate([d_gate, d_up], axis=-1).astype(jnp.bfloat16)
    d_rows = jnp.einsum(
        "shmf,hdf->shmd", d_gate_up, full_gu, preferred_element_type=jnp.float32
    ).astype(jnp.bfloat16)
    rows_back = lax.all_to_all(d_rows, "expert", split_axis=0, concat_axis=0, tiled=True)
    gathered_grads = rows_back.reshape(-1, model_width)[target_cell].reshape(
        token_count, top_count, model_width
    )
    d_tokens = jnp.sum(gathered_grads.astype(jnp.float32), axis=1).astype(jnp.bfloat16)
    part_gu = jnp.einsum("shmd,shmf->hdf", arrived, d_gate_up, preferred_element_type=jnp.float32)
    part_dn = jnp.einsum(
        "shmd,shmf->hdf", d_outputs, activation, preferred_element_type=jnp.float32
    )
    sum_gu, sum_dn = (
        lax.psum_scatter(
            part_gu.astype(jnp.bfloat16), "dp", scatter_dimension=1, tiled=True
        ).astype(jnp.float32),
        lax.psum_scatter(
            part_dn.astype(jnp.bfloat16), "dp", scatter_dimension=1, tiled=True
        ).astype(jnp.float32),
    )
    grad_gu = sum_gu.astype(jnp.bfloat16)
    grad_dn = jnp.swapaxes(sum_dn, 1, 2).astype(jnp.bfloat16)
    return (layer_out, d_tokens, grad_gu, grad_dn)


def solution(mesh):
    return jax.shard_map(
        shards,
        mesh=mesh,
        in_specs=(
            P(("groups", "expert", "dp"), None),
            P(("groups", "expert", "dp"), None),
            P(("groups", "expert", "dp"), None),
            P("expert", "dp", None),
            P("expert", None, "dp"),
            P(),
            P(("groups", "expert", "dp"), None),
        ),
        out_specs=(
            P(("groups", "expert", "dp"), None),
            P(("groups", "expert", "dp"), None),
            P(("groups", "expert"), "dp", None),
            P(("groups", "expert"), None, "dp"),
        ),
        check_vma=False,
    )
```

profile of v0, /device:TPU:29, one launch (start us, length us, event | category | flops | bytes accessed | tf_op | source)
XLA Modules:
  0.0 898.9 jit_solution(17954790021503623060)
XLA Ops:
  7.2 6.2 copy.47
  13.4 5.4 all-to-all-start.2
  18.8 0.0 all-gather.5.cloned.1.call-start
  18.9 2.0 sort.17
  20.9 0.1 reshape.106
  21.0 0.1 copy.44
  21.1 0.1 reshape.121
  21.2 133.0 %all-to-all-done.2 = bf16[16,4,64,768]{3,2,0,1:T(8,128)(2,1)} async-done(((bf16[16,4,64,768]{3,2,0,1:T(8,128)(2,1)}), bf16[16,4,64,768]{3,2,0,1:T(8,128)(2,1)}, u32[]{:S(2)}, u32[]{:S(2)}) %all-to-all-start.2) | async-done | bytes 6291488 | tf_op jit(solution)/shard_map/all_to_all | solution.py:17
  154.2 6.4 gather_fusion.1
  160.6 3.2 copy.48
  163.8 140.6 %all_to_all.60 = bf16[16,4,64,768]{3,2,0,1:T(8,128)(2,1)S(1)} all-to-all(bf16[16,4,64,768]{3,2,0,1:T(8,128)(2,1)S(1)} %copy.48), channel_id=1, replica_groups=mesh['groups'=2,'expert'=4,'dp'=4] {'expert'}, dimensions={1} | all-to-all | bytes 12582912 | tf_op jit(solution)/shard_map/all_to_all | solution.py:25
  304.5 3.1 copy.49
  307.6 0.0 all-gather.5.cloned.1.call-update
  307.6 0.0 all-gather.3.cloned.1.call-start
  307.7 1.8 copy-done.1
  309.5 0.3 copy.43
  309.7 72.8 %all_to_all.61 = bf16[16,4,96,256]{3,2,0,1:T(8,128)(2,1)S(1)} all-to-all(bf16[16,4,96,256]{3,2,0,1:T(8,128)(2,1)S(1)} %copy.43), channel_id=1, replica_groups=mesh['groups'=2,'expert'=4,'dp'=4] {'expert'}, dimensions={1} | all-to-all | bytes 6291456 | tf_op jit(solution)/shard_map/all_to_all | solution.py:18
  382.5 2.4 gather_fusion
  384.9 2.1 copy.45
  387.1 72.8 %all_to_all.62 = bf16[16,4,96,256]{3,2,0,1:T(8,128)(2,1)S(1)} all-to-all(bf16[16,4,96,256]{3,2,0,1:T(8,128)(2,1)S(1)} %copy.45), channel_id=1, replica_groups=mesh['groups'=2,'expert'=4,'dp'=4] {'expert'}, dimensions={1} | all-to-all | bytes 6291456 | tf_op jit(solution)/shard_map/all_to_all | solution.py:26
  459.8 2.0 copy.46
  461.9 0.0 all-gather.3.cloned.1.call-update
  461.9 0.7 copy-done.4
  462.6 0.1 copy.50
  462.7 0.1 eq.29
  462.8 0.1 eq.25
  462.9 18.0 %reduce-window.6 = s32[64,8,128]{2,1,0:T(8,128)S(1)} reduce-window(s32[64,8,128]{2,1,0:T(8,128)S(1)} %fusion.31, s32[]{:T(128)} %constant.11.clone.1), window={size=1x1x128 pad=0_0x0_0x127_0}, to_apply=%region_2.3 | reduce-window | flops 8323072 | bytes 524292 | tf_op jit(solution)/shard_map/reduce-window
  480.9 0.1 slice.30
  481.0 0.1 copy.52
  481.2 0.1 copy.53
  481.3 0.1 broadcast_add_fusion
  481.5 0.1 select_reduce_fusion
  481.6 4.3 scatter_custom_fusion
  486.0 5.3 gather_fusion.2
  491.3 5.8 all-to-all-start.4
  497.1 0.1 copy.42
  497.2 0.1 reshape.114
  497.4 6.2 gather_fusion.4
  503.5 0.1 mul.60
  503.6 4.1 gather_fusion.5
  507.7 1.8 fusion.8
  509.5 32.1 %all-to-all-done.4 = bf16[4,16,16,1024]{3,2,1,0:T(8,128)(2,1)} async-done(((bf16[4,16,16,1024]{3,2,1,0:T(8,128)(2,1)}), bf16[4,16,16,1024]{3,2,1,0:T(8,128)(2,1)}, u32[]{:S(2)}, u32[]{:S(2)}) %all-to-all-start.4) | async-done | bytes 2097184 | tf_op jit(solution)/shard_map/all_to_all | solution.py:70
  541.6 7.1 all-to-all-start.6
  548.6 12.6 %fusion.12 = f32[4,16,16,768]{3,2,0,1:T(8,128)} fusion(bf16[4,16,16,1024]{3,2,1,0:T(8,128)(2,1)} %all-to-all-done.4, bf16[16,1024,768]{2,1,0:T(8,128)(2,1)} %all-gather.5.cloned.1.call-done), kind=kOutput, calls=%fused_computation.27 | convolution fusion | flops 1610612736 | bytes 30408704 | tf_op jit(solution)/shard_map/shmd,hdf->shmf/dot_general | solution.py:73
  561.3 32.2 %all-to-all-done.6 = bf16[4,16,16,1024]{3,2,1,0:T(8,128)(2,1)S(1)} async-done(((bf16[4,16,16,1024]{3,2,1,0:T(8,128)(2,1)}), bf16[4,16,16,1024]{3,2,1,0:T(8,128)(2,1)S(1)}, u32[]{:S(2)}, u32[]{:S(2)}) %all-to-all-start.6) | async-done | bytes 2097184 | tf_op jit(solution)/shard_map/all_to_all | solution.py:89
  593.4 10.6 %fusion.23 = (bf16[4,16,16,384]{3,2,0,1:T(8,128)(2,1)S(1)}, bf16[4,16,16,384]{3,2,0,1:T(8,128)(2,1)}, bf16[4,16,16,384]{3,2,0,1:T(8,128)(2,1)}) fusion(f32[4,16,16,768]{3,2,0,1:T(8,128)} %fusion.12, bf16[4,16,16,1024]{3,2,1,0:T(8,128)(2,1)S(1)} %all-to-all-done.6, bf16[16,384,1024]{2,1,0:T(8,128)(2,1)} %all-gather.3.cloned.1.call-done), kind=kOutput, calls=%fused_computation.33 | convolution fusion | flops 811204608 | bytes 20185088 | tf_op jit(solution)/shard_map/shmd,hfd->shmf/dot_general | solution.py:92
  604.0 7.5 bitcast_convert_fusion.1
  611.5 0.0 reduce-scatter.3.cloned.1.call-start
  611.6 1.1 copy-done.7
  612.6 16.7 %bitcast_convert_fusion = bf16[16,1024,768]{2,1,0:T(8,128)(2,1)} fusion(bf16[4,16,16,1024]{3,2,1,0:T(8,128)(2,1)} %all-to-all-done.4, bf16[4,16,16,384]{3,2,0,1:T(8,128)(2,1)S(1)} %copy-done.7, bf16[4,16,16,384]{3,2,0,1:T(8,128)(2,1)S(1)} %get-tuple-element.24), kind=kOutput, calls=%fused_computation.8 | convolution fusion | flops 1626341376 | bytes 28835840 | tf_op jit(solution)/shard_map/shmd,shmf->hdf/dot_general | solution.py:104
  629.3 8.6 convert_bitcast_fusion.1
  637.9 1.5 copy.55
  639.4 6.5 all-to-all-start.5
  646.0 13.6 %convert_bitcast_fusion = bf16[4,16,16,1024]{3,2,0,1:T(8,128)(2,1)} fusion(bf16[16,1024,768]{2,1,0:T(8,128)(2,1)} %all-gather.5.cloned.1.call-done, bf16[4,16,16,384]{3,2,0,1:T(8,128)(2,1)} %get-tuple-element.25, bf16[4,16,16,384]{3,2,0,1:T(8,128)(2,1)S(1)} %get-tuple-element.24), kind=kOutput, calls=%fused_computation.25 | convolution fusion | flops 1614807040 | bytes 28835840 | tf_op jit(solution)/shard_map/shmf,hdf->shmd/dot_general | solution.py:96
  659.5 3.2 copy.58
  662.8 28.8 %all-to-all-done.5 = bf16[4,16,16,1024]{3,2,1,0:T(8,128)(2,1)S(1)} async-done(((bf16[4,16,16,1024]{3,2,1,0:T(8,128)(2,1)}), bf16[4,16,16,1024]{3,2,1,0:T(8,128)(2,1)S(1)}, u32[]{:S(2)}, u32[]{:S(2)}) %all-to-all-start.5) | async-done | bytes 2097184 | tf_op jit(solution)/shard_map/all_to_all | solution.py:82
  691.6 6.5 all-to-all-start.7
  698.1 5.3 gather_fusion.3
  703.5 39.5 %all-to-all-done.7 = bf16[4,16,16,1024]{3,2,1,0:T(8,128)(2,1)} async-done(((bf16[4,16,16,1024]{3,2,1,0:T(8,128)(2,1)}), bf16[4,16,16,1024]{3,2,1,0:T(8,128)(2,1)}, u32[]{:S(2)}, u32[]{:S(2)}) %all-to-all-start.7) | async-done | bytes 2097184 | tf_op jit(solution)/shard_map/all_to_all | solution.py:99
  743.0 7.6 gather_fusion.6
  750.6 2.1 bitcast_reduce_fusion
  752.7 2.1 fusion.9
  754.8 4.8 copy.61
  759.6 132.8 %reduce-scatter.3.cloned.1.call-done = bf16[16,256,768]{2,1,0:T(8,128)(2,1)} async-done(((bf16[16,1024,768]{2,1,0:T(8,128)(2,1)}), bf16[16,256,768]{2,1,0:T(8,128)(2,1)}) %reduce-scatter.3.cloned.1.call-update) | async-done | bytes 6291472 | tf_op jit(solution)/shard_map/reduce_scatter | solution.py:109
  (33 shorter events, 0.2 us)
Async XLA Ops:
  13.4 5.5 copy-start.6
  13.4 140.8 %all-to-all-start.2 = ((bf16[16,4,64,768]{3,2,0,1:T(8,128)(2,1)}), bf16[16,4,64,768]{3,2,0,1:T(8,128)(2,1)}, u32[]{:S(2)}, u32[]{:S(2)}) async-start(bf16[16,4,64,768]{3,2,0,1:T(8,128)(2,1)} %copy.47), calls=%async_computation.2 | async-start | bytes 12582912 | tf_op jit(solution)/shard_map/all_to_all | solution.py:17
  18.8 529.8 %all-gather.5.cloned.1.call-start = ((), (), s32[]{:S(2)}) async-start(), calls=%async_computation.11 | async-start | bytes 31457280 | tf_op jit(solution)/shard_map/all_gather | solution.py:59
  307.6 1.9 copy-start.1
  307.6 285.8 %all-gather.3.cloned.1.call-start = ((), (), s32[]{:S(2)}) async-start(), calls=%async_computation.10 | async-start | bytes 15728640 | tf_op jit(solution)/shard_map/all_gather | solution.py:60
  461.9 0.7 copy-start.4
  461.9 19.4 %copy-start.2 = (bf16[128,1024]{1,0:T(8,128)(2,1)S(1)}, bf16[128,1024]{1,0:T(8,128)(2,1)}, u32[]{:S(2)}) copy-start(bf16[128,1024]{1,0:T(8,128)(2,1)} %param.7) | copy-start | bytes 786436
  491.3 5.8 copy-start.5
  491.3 50.3 %all-to-all-start.4 = ((bf16[4,16,16,1024]{3,2,1,0:T(8,128)(2,1)}), bf16[4,16,16,1024]{3,2,1,0:T(8,128)(2,1)}, u32[]{:S(2)}, u32[]{:S(2)}) async-start(bf16[4,16,16,1024]{3,2,1,0:T(8,128)(2,1)} %bitcast.21), calls=%async_computation.4 | async-start | bytes 4194304 | tf_op jit(solution)/shard_map/all_to_all | solution.py:70
  497.3 6.2 copy-start.3
  541.6 51.9 %all-to-all-start.6 = ((bf16[4,16,16,1024]{3,2,1,0:T(8,128)(2,1)}), bf16[4,16,16,1024]{3,2,1,0:T(8,128)(2,1)S(1)}, u32[]{:S(2)}, u32[]{:S(2)}) async-start(bf16[4,16,16,1024]{3,2,1,0:T(8,128)(2,1)} %fusion.8), calls=%async_computation.6 | async-start | bytes 4194304 | tf_op jit(solution)/shard_map/all_to_all | solution.py:89
  548.6 206.2 %reduce-scatter.5.cloned.1.call-start = ((), (), s32[]{:S(2)}) async-start(), calls=%async_computation.13 | async-start | bytes 15728640 | tf_op jit(solution)/shard_map/reduce_scatter | solution.py:112
  611.5 1.1 copy-start.7
  611.5 280.9 %reduce-scatter.3.cloned.1.call-start = ((), (), s32[]{:S(2)}) async-start(), calls=%async_computation.12 | async-start | bytes 31457280 | tf_op jit(solution)/shard_map/reduce_scatter | solution.py:109
  639.4 52.2 %all-to-all-start.5 = ((bf16[4,16,16,1024]{3,2,1,0:T(8,128)(2,1)}), bf16[4,16,16,1024]{3,2,1,0:T(8,128)(2,1)S(1)}, u32[]{:S(2)}, u32[]{:S(2)}) async-start(bf16[4,16,16,1024]{3,2,1,0:T(8,128)(2,1)} %copy.55), calls=%async_computation.5 | async-start | bytes 4194304 | tf_op jit(solution)/shard_map/all_to_all | solution.py:82
  691.6 51.4 %all-to-all-start.7 = ((bf16[4,16,16,1024]{3,2,1,0:T(8,128)(2,1)}), bf16[4,16,16,1024]{3,2,1,0:T(8,128)(2,1)}, u32[]{:S(2)}, u32[]{:S(2)}) async-start(bf16[4,16,16,1024]{3,2,1,0:T(8,128)(2,1)} %copy.58), calls=%async_computation.7 | async-start | bytes 4194304 | tf_op jit(solution)/shard_map/all_to_all | solution.py:99
  750.6 2.1 copy-start
Sparse Core Ops, SparseCore 0:
  307.7 156.2 all-gather.4
  465.6 83.7 all-gather.2
  611.6 101.8 reduce-scatter.4
  716.6 175.7 reduce-scatter.2
where the time goes:
time: 902 us; the launch traced here: 899 us
  waiting for transfers between devices  399 us (44%)
  blocking collectives  286 us (32%)
  local copies, waits for them, and re-layouts  72.9 us (8%)
  matrix products  69.5 us (8%)
  starting transfers between devices  31.5 us (3%)
  other arithmetic  26.3 us (3%)
  between operations  14 us (2%)
    all_to_all x1, blocking collectives, relocate(): lax.all_to_all(pick_gu, 'expert', split_axis=1, concat_axis=1, tiled=True)  141 us
    all_to_all x1, waiting for transfers between devices, relocate(): lax.all_to_all(spread_gu, 'expert', split_axis=1, concat_axis=0, tiled=True)  133 us
    reduce_scatter x1, waiting for transfers between devices, shards(): lax.psum_scatter(part_gu.astype(jnp.bfloat16), 'dp', scatter_dimension=1,...  133 us
    all_to_all x1, blocking collectives, relocate(): lax.all_to_all(spread_dn, 'expert', split_axis=1, concat_axis=0, tiled=True)  72.8 us
    all_to_all x1, blocking collectives, relocate(): lax.all_to_all(pick_dn, 'expert', split_axis=1, concat_axis=1, tiled=True)  72.8 us
    all_to_all x1, waiting for transfers between devices, shards(): lax.all_to_all(d_rows, 'expert', split_axis=0, concat_axis=0, tiled=True)  39.5 us
    all_to_all x1, waiting for transfers between devices, shards(): lax.all_to_all(scaled_cot.reshape(row_shape), 'expert', split_axis=0, con...  32.2 us
    all_to_all x1, waiting for transfers between devices, shards(): lax.all_to_all(outgoing.reshape(row_shape), 'expert', split_axis=0, conca...  32.1 us
  transfers between devices with their start and end apart: 9, of which 6 were waited for; matrix products, arithmetic and copies ran while one was open for 14% of the time, Pallas kernels for 0%

commit v1 on v0

--- a/solution.py
+++ b/solution.py
@@ -1,6 +1,10 @@
+import functools
+
 import jax
 import jax.numpy as jnp
 from jax import lax
+from jax.experimental import pallas as pl
+from jax.experimental.pallas import tpu as pltpu
 from jax.sharding import PartitionSpec as P
 
 MOST = 16
@@ -46,7 +50,7 @@
     return (target_cell, source)
 
 
-def shards(tokens, expert_ids, gate_values, w_gate_up, w_down, new_slot, cotangent):
+def by_rows(tokens, expert_ids, gate_values, w_gate_up, w_down, new_slot, cotangent):
     expert_peers = lax.axis_size("expert")
     home_slots = w_gate_up.shape[0]
     model_width = tokens.shape[1]
@@ -118,6 +122,263 @@
     return (layer_out, d_tokens, grad_gu, grad_dn)
 
 
+BF16, F32 = jnp.bfloat16, jnp.float32
+
+
+def contract(a, b, dim_a, dim_b):
+    return lax.dot_general(a, b, (((dim_a,), (dim_b,)), ((), ())), preferred_element_type=F32)
+
+
+def swap(array, axis, offset):
+    size = lax.axis_size(axis)
+    return lax.ppermute(array, axis, [(p, p ^ offset) for p in range(size)])
+
+
+def shift(array, axis, offset):
+    size = lax.axis_size(axis)
+    return lax.ppermute(array, axis, [(p, (p + offset) % size) for p in range(size)])
+
+
+def partial_kernel(x_ref, c_ref, gu_ref, dn_ref, *outs):
+    peers, _, rows, width = x_ref.shape
+    split = gu_ref.shape[2]
+    gate_up = contract(x_ref[...].reshape(peers * rows, width), gu_ref[0], 1, 0)
+    d_act = contract(c_ref[...].reshape(peers * rows, width), dn_ref[0], 1, 1)
+    for j, out in enumerate(outs):
+        out[0, :, :split] = gate_up[j * rows : (j + 1) * rows].astype(out.dtype)
+        out[0, :, split:] = d_act[j * rows : (j + 1) * rows].astype(out.dtype)
+
+
+def partial_products(x, c, w_gate_up, w_down, first, count):
+    peers, _, rows, width = x.shape
+    hidden = w_down.shape[1]
+    row_spec = pl.BlockSpec((peers, 1, rows, width), lambda s: (0, s + first, 0, 0))
+    dtypes = [BF16 if j & 1 else F32 for j in range(peers)]
+    return pl.pallas_call(
+        partial_kernel,
+        grid=(count,),
+        in_specs=[
+            row_spec,
+            row_spec,
+            pl.BlockSpec((1, width, 2 * hidden), lambda s: (s + first, 0, 0)),
+            pl.BlockSpec((1, hidden, width), lambda s: (s + first, 0, 0)),
+        ],
+        out_specs=[pl.BlockSpec((1, rows, 3 * hidden), lambda s: (s, 0, 0)) for _ in dtypes],
+        out_shape=[jax.ShapeDtypeStruct((count, rows, 3 * hidden), t) for t in dtypes],
+        cost_estimate=pl.CostEstimate(
+            flops=2 * count * peers * rows * width * 3 * hidden,
+            bytes_accessed=count * (3 * hidden * width * 2 + peers * rows * (3 * hidden * 3 + width * 4)),
+            transcendentals=0,
+        ),
+    )(x, c, w_gate_up, w_down)
+
+
+def back_kernel(*refs):
+    *mids, gate_ref, gu_ref, dn_ref, out_ref, grad_ref = refs
+    hidden = dn_ref.shape[1]
+    mid = jnp.concatenate([m[0] for m in mids], axis=0)
+    out = contract(mid[:, :hidden], dn_ref[0], 1, 0)
+    out_ref[0] = (gate_ref[0] * out).astype(BF16)
+    grad_ref[0] = contract(mid[:, hidden:], gu_ref[0], 1, 1).astype(BF16)
+
+
+def back_products(mids, gates, w_gate_up, w_down, first):
+    count, rows, wide = mids[0].shape
+    hidden, width = w_down.shape[1:]
+    total = rows * len(mids)
+    out_spec = pl.BlockSpec((1, total, width), lambda s: (s, 0, 0))
+    return pl.pallas_call(
+        back_kernel,
+        grid=(count,),
+        in_specs=[pl.BlockSpec((1, rows, wide), lambda s: (s, 0, 0)) for _ in mids]
+        + [
+            pl.BlockSpec((1, total, 1), lambda s: (s + first, 0, 0)),
+            pl.BlockSpec((1, width, 2 * hidden), lambda s: (s + first, 0, 0)),
+            pl.BlockSpec((1, hidden, width), lambda s: (s + first, 0, 0)),
+        ],
+        out_specs=[out_spec, out_spec],
+        out_shape=[jax.ShapeDtypeStruct((count, total, width), BF16)] * 2,
+        cost_estimate=pl.CostEstimate(
+            flops=2 * count * total * width * wide,
+            bytes_accessed=count * 2 * (wide * width + total * (wide + 2 * width)),
+            transcendentals=0,
+        ),
+    )(*mids, gates, w_gate_up, w_down)
+
+
+def combine_kernel(one_ref, out_ref, grad_ref, sum_ref):
+    slots, most, tokens = one_ref.shape[2:]
+    one = one_ref[...].reshape(slots * most, tokens)
+    width = out_ref.shape[-1]
+    sum_ref[0, 0, 0] = contract(one, out_ref[...].reshape(slots * most, width), 0, 0).astype(BF16)
+    sum_ref[0, 0, 1] = contract(one, grad_ref[...].reshape(slots * most, width), 0, 0).astype(BF16)
+
+
+def combine(one, out_rows, grad_rows):
+    far, near, slots, most, tokens = one.shape
+    width = out_rows.shape[-1]
+    shape = (slots, near, far, most, width)
+    row_spec = pl.BlockSpec((slots, 1, 1, most, width), lambda k, j: (0, j, k, 0, 0))
+    return pl.pallas_call(
+        combine_kernel,
+        grid=(far, near),
+        in_specs=[
+            pl.BlockSpec((1, 1, slots, most, tokens), lambda k, j: (k, j, 0, 0, 0)),
+            row_spec,
+            row_spec,
+        ],
+        out_specs=pl.BlockSpec((1, 1, 2, tokens, width), lambda k, j: (k, j, 0, 0, 0)),
+        out_shape=jax.ShapeDtypeStruct((far, near, 2, tokens, width), BF16),
+    )(one, out_rows.reshape(shape), grad_rows.reshape(shape))
+
+
+def grads_kernel(x_ref, c_ref, *refs):
+    *mids, gu_ref, dn_ref = refs
+    peers, _, rows, width = x_ref.shape
+    hidden = dn_ref.shape[1]
+    mid = jnp.concatenate([m[0] for m in mids], axis=0)
+    gu_ref[0] = contract(x_ref[...].reshape(peers * rows, width), mid[:, hidden:], 0, 0).astype(BF16)
+    dn_ref[0] = contract(mid[:, :hidden], c_ref[...].reshape(peers * rows, width), 0, 0).astype(BF16)
+
+
+def weight_grads(x, c, mids):
+    peers, slots, rows, width = x.shape
+    most, wide = mids[0].shape[1:]
+    hidden = wide // 3
+    row_spec = pl.BlockSpec((peers, 1, rows, width), lambda s: (0, s, 0, 0))
+    return pl.pallas_call(
+        grads_kernel,
+        grid=(slots,),
+        in_specs=[row_spec, row_spec]
+        + [pl.BlockSpec((1, most, wide), lambda s: (s, 0, 0)) for _ in mids],
+        out_specs=[
+            pl.BlockSpec((1, width, 2 * hidden), lambda s: (s, 0, 0)),
+            pl.BlockSpec((1, hidden, width), lambda s: (s, 0, 0)),
+        ],
+        out_shape=[
+            jax.ShapeDtypeStruct((slots, width, 2 * hidden), BF16),
+            jax.ShapeDtypeStruct((slots, hidden, width), BF16),
+        ],
+    )(x, c, *mids)
+
+
+def route(ids, gates, chosen):
+    tokens = ids.shape[-1]
+    match = ids[:, :, None] == chosen[None, None, :, None, None]
+    hit = jnp.any(match, axis=3)
+    gate = jnp.sum(jnp.where(match, gates[:, :, None], 0.0), axis=3)
+    earlier = jnp.triu(jnp.ones((tokens, tokens), BF16), 1)
+    place = jnp.einsum("kjst,tu->kjsu", hit.astype(BF16), earlier, preferred_element_type=F32)
+    cell = jnp.arange(MOST, dtype=jnp.int32)[None, None, None, :, None]
+    one = hit[:, :, :, None] & (place.astype(jnp.int32)[:, :, :, None] == cell)
+    row_gate = jnp.sum(jnp.where(one, gate[:, :, :, None], 0.0), axis=-1)
+    return one.astype(BF16), row_gate.transpose(2, 1, 0, 3)
+
+
+def select(one, row_gate, tokens, cotangent):
+    far, near, slots, most, _ = one.shape
+    shape = (near, slots, far * most, tokens.shape[-1])
+    x = jnp.einsum("kjsmt,kjtd->jskmd", one, tokens, preferred_element_type=F32).astype(BF16)
+    c = jnp.einsum("kjsmt,kjtd->jskmd", one, cotangent, preferred_element_type=F32)
+    c = (row_gate.swapaxes(0, 1)[..., None] * c).astype(BF16)
+    return x.reshape(shape), c.reshape(shape)
+
+
+def by_slices(tokens, expert_ids, gate_values, w_gate_up, w_down, new_slot, cotangent, chunks=1):
+    far, near = lax.axis_size("expert"), lax.axis_size("dp")
+    here, lane = lax.axis_index("expert"), lax.axis_index("dp")
+    slots, width, wide = w_gate_up.shape
+    hidden = wide // 2
+    count, top = expert_ids.shape
+    bits = [1 << b for b in range(near.bit_length() - 1)]
+
+    info = jnp.concatenate([expert_ids.T.astype(F32), gate_values.T], axis=0)
+    info = lax.all_gather(info, ("expert", "dp"), axis=0)
+    order = (here - jnp.arange(far)[:, None]) % far * near + (lane ^ jnp.arange(near)[None, :])
+    info = info[order]
+    ids, gates = info[:, :, :top].astype(jnp.int32), info[:, :, top:]
+
+    pair = jnp.stack([tokens, cotangent]).reshape(2, count, near, width).transpose(2, 0, 1, 3)
+    pieces = []
+    for j in range(near):
+        piece = lax.dynamic_index_in_dim(pair, lane ^ j, 0, keepdims=False)
+        pieces.append(swap(piece, "dp", j) if j else piece)
+    blocks = [jnp.stack(pieces)]
+    for _ in range(far - 1):
+        blocks.append(shift(blocks[-1], "expert", 1))
+    blocks = jnp.stack(blocks)
+    all_tokens, all_cot = blocks[:, :, 0], blocks[:, :, 1]
+
+    one, row_gate = route(ids, gates, here * slots + jnp.arange(slots))
+    x, c = select(one, row_gate, all_tokens, all_cot)
+    gate_column = row_gate.reshape(slots, near * far * MOST, 1)
+
+    step = slots // chunks
+    home = [[None] * chunks for _ in range(far)]
+    out_rows, grad_rows = [], []
+    for n in range(chunks):
+        parts = list(partial_products(x, c, w_gate_up, w_down, n * step, step))
+        for bit in bits:
+            for j in range(0, near, 2 * bit):
+                got = swap(parts[j + bit].astype(BF16), "dp", bit)
+                parts[j] = parts[j].astype(F32) + got.astype(F32)
+        gate, up, d_act = (parts[0][..., p * hidden : (p + 1) * hidden] for p in range(3))
+        sigmoid = jax.nn.sigmoid(gate)
+        silu = gate * sigmoid
+        mid = jnp.concatenate(
+            [silu * up, d_act * up * sigmoid * (1.0 + gate * (1.0 - sigmoid)), d_act * silu],
+            axis=-1,
+        ).astype(BF16)
+        by_home = mid.reshape(step, far, MOST, 3 * hidden)
+        for k in range(far):
+            home[k][n] = shift(by_home[:, k], "expert", -k) if k else by_home[:, k]
+        mids = {0: mid}
+        for bit in reversed(bits):
+            for j in list(mids):
+                mids[j + bit] = swap(mids[j], "dp", bit)
+        mids = [mids[j] for j in range(near)]
+        out, grad = back_products(mids, gate_column, w_gate_up, w_down, n * step)
+        out_rows.append(out)
+        grad_rows.append(grad)
+
+    held = jnp.concatenate([home[k][n] for k in range(far) for n in range(chunks)], axis=0)
+    experts = far * slots
+    numbers = jnp.arange(experts, dtype=jnp.int32)
+    inverse = jnp.sum(jnp.where(new_slot[None, :] == numbers[:, None], numbers[None, :], 0), axis=1)
+    moved = {}
+    for k in range(far):
+        chosen = inverse[(here + k) % far * slots + jnp.arange(slots)]
+        place = (chosen // slots - here) % far * slots + chosen % slots
+        picked = held[place]
+        moved[k, 0] = shift(picked, "expert", k) if k else picked
+    for bit in reversed(bits):
+        for k, j in list(moved):
+            moved[k, j + bit] = swap(moved[k, j], "dp", bit)
+
+    one_new, gate_new = route(ids, gates, inverse[here * slots + jnp.arange(slots)])
+    x_new, c_new = select(one_new, gate_new, all_tokens, all_cot)
+    d_gate_up, d_down = weight_grads(
+        x_new, c_new, [moved[k, j] for j in range(near) for k in range(far)]
+    )
+
+    sums = combine(one, jnp.concatenate(out_rows), jnp.concatenate(grad_rows))
+    total = sums[1 % far]
+    for k in range(1, far):
+        got = shift(total, "expert", 1)
+        total = (got.astype(F32) + sums[(k + 1) % far].astype(F32)).astype(BF16)
+    pieces = [swap(total[j], "dp", j) if j else total[j] for j in range(near)]
+    whole = jnp.stack(pieces)[lane ^ jnp.arange(near)]
+    whole = whole.transpose(1, 2, 0, 3).reshape(2, count, near * width)
+    return whole[0], whole[1], d_gate_up, d_down
+
+
+def shards(tokens, expert_ids, *rest):
+    far, near = lax.axis_size("expert"), lax.axis_size("dp")
+    if far <= expert_ids.shape[1] and near & (near - 1) == 0:
+        return by_slices(tokens, expert_ids, *rest)
+    return by_rows(tokens, expert_ids, *rest)
+
+
 def solution(mesh):
     return jax.shard_map(
         shards,

time: 902 us -> 423 us (0.47)
  blocking collectives: 286 us -> 24.3 us
  waiting for transfers between devices: 399 us -> 212 us
  matrix products: 69.5 us -> 3.95 us
  Pallas kernels: 0 us -> 60.3 us
  local copies, waits for them, and re-layouts: 72.9 us -> 30.3 us
  starting transfers between devices: 31.5 us -> 69.5 us
  between operations: 14 us -> 1.33 us
    all_to_all x3 -> x0, blocking collectives: 286 us -> none  [the longest x1 141 us: relocate(): lax.all_to_all(pick_gu, 'expert', split_axis=1, concat_axis=1, tiled=True)]
    all_to_all x5 -> x0, waiting for transfers between devices: 266 us -> none  [the longest x1 133 us: relocate(): lax.all_to_all(spread_gu, 'expert', split_axis=1, concat_axis=0, tiled=True)]
    ppermute x0 -> x36, waiting for transfers between devices: none -> 212 us  [the longest x24 143 us: swap(): return lax.ppermute(array, axis, [(p, p ^ offset) for p in range(size)])]
    reduce_scatter x2 -> x0, waiting for transfers between devices: 133 us -> none  [the longest x1 133 us: shards(): lax.psum_scatter(part_gu.astype(jnp.bfloat16), 'dp', scatter_dimension=1,...]
    ppermute x0 -> x36, starting transfers between devices: none -> 69.5 us  [the longest x12 47.9 us: shift(): lax.ppermute(array, axis, [(p, (p + offset) % size) for p in range(size)])]
    dot_general x6, matrix products: 69.5 us -> 3.95 us  [the longest x2 1.48 us: select(): jnp.einsum('kjsmt,kjtd->jskmd', one, cotangent, preferred_element_type=F32)]
    pallas_call x0 -> x4, Pallas kernels: none -> 60.3 us  [the longest x1 17.5 us: partial_products(): pl.pallas_call(partial_kernel, grid=(count,), in_specs=[row_spec, row_spe...]
    gather x9 -> x11, local copies, waits for them, and re-layouts: 42.7 us -> 9.09 us  [the longest x4 4.15 us: by_slices(): picked = held[place]]
  transfers between devices with their start and end apart: 9 -> 36, of which waited for: 6 -> 13; matrix products, arithmetic and copies ran while one was open for 14% -> 9% of each run, Pallas kernels for 0% -> 10%
where the time goes in v1:
time: 423 us; the launch traced here: 421 us
  waiting for transfers between devices  212 us (50%)
  starting transfers between devices  69.5 us (16%)
  Pallas kernels  60.3 us (14%)
  local copies, waits for them, and re-layouts  30.3 us (7%)
  blocking collectives  24.3 us (6%)
  other arithmetic  20 us (5%)
    ppermute x24, waiting for transfers between devices, swap(): return lax.ppermute(array, axis, [(p, p ^ offset) for p in range(size)])  143 us
    ppermute x12, waiting for transfers between devices, shift(): lax.ppermute(array, axis, [(p, (p + offset) % size) for p in range(size)])  68.7 us
    ppermute x12, starting transfers between devices, shift(): lax.ppermute(array, axis, [(p, (p + offset) % size) for p in range(size)])  47.9 us
    all_gather x1, blocking collectives, by_slices(): info = lax.all_gather(info, ('expert', 'dp'), axis=0)  24.3 us
    ppermute x24, starting transfers between devices, swap(): return lax.ppermute(array, axis, [(p, p ^ offset) for p in range(size)])  21.5 us
    pallas_call x1, Pallas kernels, partial_products(): pl.pallas_call(partial_kernel, grid=(count,), in_specs=[row_spec, row_spe...  17.5 us
    pallas_call x1, Pallas kernels, weight_grads(): pl.pallas_call(grads_kernel, grid=(slots,), in_specs=[row_spec, row_spec]...  15.8 us
    pallas_call x1, Pallas kernels, back_products(): pl.pallas_call(back_kernel, grid=(count,), in_specs=[pl.BlockSpec((1, row...  15.4 us
  transfers between devices with their start and end apart: 36, of which 13 were waited for; matrix products, arithmetic and copies ran while one was open for 9% of the time, Pallas kernels for 10%

profile of v1, /device:TPU:29, one launch (start us, length us, event | category | flops | bytes accessed | tf_op | source)
XLA Modules:
  0.0 421.4 jit_solution(6648653058762038256)
XLA Ops:
  0.7 1.1 stack.49
  1.9 1.1 stack.50
  3.1 1.8 collective-permute-start.2
  5.6 3.6 collective-permute-done.2
  9.2 2.8 collective-permute-done.1
  12.2 24.3 %all-gather = f32[256,128]{1,0:T(8,128)S(1)} all-gather(f32[16,128]{1,0:T(8,128)S(1)} %pad_maximum_fusion.6), channel_id=2, replica_groups=mesh['groups'=2,'expert'=4,'dp'=4] {'expert','dp'}, dimensions={0}, use_global_device_ids=true | all-gather | bytes 139264 | tf_op jit(solution)/shard_map/all_gather | solution.py:296
  37.2 4.8 %collective-permute-start.4 = (bf16[4,2,128,256]{3,2,0,1:T(8,128)(2,1)S(1)}, bf16[4,2,128,256]{3,2,0,1:T(8,128)(2,1)S(1)}, u32[]{:S(2)}, u32[]{:S(2)}) collective-permute-start(bf16[4,2,128,256]{3,2,0,1:T(8,128)(2,1)S(1)} %collective-permute-done.3), channel_id=1, source_target_pairs={{0,4},{4,8},{8,12},{12,0},{1,5},{5,9},{9,13},{13,1},{2,6},{6,10},{... | collective-permute-start | bytes 1572872 | tf_op jit(solution)/shard_map/ppermute | solution.py:139
  42.7 1.4 compare_reduce_fusion
  44.3 8.9 %collective-permute-done.4 = bf16[4,2,128,256]{3,2,0,1:T(8,128)(2,1)S(1)} collective-permute-done((bf16[4,2,128,256]{3,2,0,1:T(8,128)(2,1)S(1)}, bf16[4,2,128,256]{3,2,0,1:T(8,128)(2,1)S(1)}, u32[]{:S(2)}, u32[]{:S(2)}) %collective-permute-start.4) | collective-permute-done | bytes 524320 | tf_op jit(solution)/shard_map/ppermute | solution.py:139
  53.2 4.0 collective-permute-start.5
  57.2 1.1 fusion.10
  58.3 0.8 select_reduce_fusion.1
  59.1 1.6 fusion.2
  60.7 6.7 %collective-permute-done.5 = bf16[4,2,128,256]{3,2,0,1:T(8,128)(2,1)S(1)} collective-permute-done((bf16[4,2,128,256]{3,2,0,1:T(8,128)(2,1)S(1)}, bf16[4,2,128,256]{3,2,0,1:T(8,128)(2,1)S(1)}, u32[]{:S(2)}, u32[]{:S(2)}) %collective-permute-start.5) | collective-permute-done | bytes 524320 | tf_op jit(solution)/shard_map/ppermute | solution.py:139
  68.4 1.6 copy.80
  70.7 1.6 copy.83
  72.3 17.5 %shard_map.102 = (f32[16,64,1152]{2,1,0:T(8,128)}, bf16[16,64,1152]{2,1,0:T(8,128)(2,1)}, f32[16,64,1152]{2,1,0:T(8,128)}, bf16[16,64,1152]{2,1,0:T(8,128)(2,1)}) custom-call(bf16[4,16,64,256]{3,2,1,0:T(8,128)(2,1)} %bitcast.206, bf16[4,16,64,256]{3,2,1,0:T(8,128)(2,1)} %bitcast.207, bf16[16,256,768]{2,1,0:T(8,128)(2,1)} %refs_5_.1, ...), custom_call_target="tpu_custom_call" | custom-call | flops 2415919104 | bytes 27787264 | tf_op jit(solution)/shard_map/pallas_call | solution.py:157
  89.8 1.9 collective-permute-start.7
  91.8 4.3 %collective-permute-done.7 = bf16[16,64,1152]{2,1,0:T(8,128)(2,1)S(1)} collective-permute-done((bf16[16,64,1152]{2,1,0:T(8,128)(2,1)}, bf16[16,64,1152]{2,1,0:T(8,128)(2,1)S(1)}, u32[]{:S(2)}, u32[]{:S(2)}) %collective-permute-start.7) | collective-permute-done | bytes 2359328 | tf_op jit(solution)/shard_map/ppermute | solution.py:134
  96.1 3.2 add_convert_fusion
  99.6 52.2 %collective-permute-done.8 = bf16[16,64,1152]{2,1,0:T(8,128)(2,1)S(1)} collective-permute-done((bf16[16,64,1152]{2,1,0:T(8,128)(2,1)S(1)}, bf16[16,64,1152]{2,1,0:T(8,128)(2,1)S(1)}, u32[]{:S(2)}, u32[]{:S(2)}) %collective-permute-start.8) | collective-permute-done | bytes 2359328 | tf_op jit(solution)/shard_map/ppermute | solution.py:134
  152.6 0.9 multiply_convert_fusion.2
  154.8 1.0 copy.84
  156.5 1.6 collective-permute-start.9
  158.1 48.3 %collective-permute-done.10.refs_2_ = bf16[16,64,1152]{2,1,0:T(8,128)(2,1)} collective-permute-done((bf16[16,64,1152]{2,1,0:T(8,128)(2,1)S(1)}, bf16[16,64,1152]{2,1,0:T(8,128)(2,1)}, u32[]{:S(2)}, u32[]{:S(2)}) %collective-permute-start.10) | collective-permute-done | bytes 2359328 | tf_op jit(solution)/shard_map/ppermute | solution.py:134
  206.3 2.1 collective-permute-start.11
  210.4 1.6 pad_maximum_fusion.1
  212.0 1.2 slice_bitcast_fusion.9
  213.3 4.0 collective-permute-start.20
  217.5 3.3 reshape.831.refs_4_
  220.8 1.2 gather_fusion.9
  222.6 15.4 %shard_map.103 = (bf16[16,256,256]{2,1,0:T(8,128)(2,1)}, bf16[16,256,256]{2,1,0:T(8,128)(2,1)}) custom-call(bf16[16,64,1152]{2,1,0:T(8,128)(2,1)} %copy-done, bf16[16,64,1152]{2,1,0:T(8,128)(2,1)} %collective-permute-done.9.refs_1_, bf16[16,64,1152]{2,1,0:T(8,128)(2,1)} %collective-permute-done.10.refs_2_, ...), custom_call_target="tpu_custom_call" | custom-call | flops 2415919104 | bytes 23068672 | tf_op jit(solution)/shard_map/pallas_call | solution.py:190
  238.0 11.6 %shard_map.104 = bf16[4,4,2,128,256]{4,3,2,1,0:T(8,128)(2,1)} custom-call(bf16[4,4,16,16,128]{4,3,2,1,0:T(8,128)(2,1)} %get-tuple-element.56.one_ref, bf16[16,4,4,16,256]{4,3,2,1,0:T(8,128)(2,1)} %bitcast.213, bf16[16,4,4,16,256]{4,3,2,1,0:T(8,128)(2,1)} %bitcast.214), custom_call_target="tpu_custom_call" | custom-call | tf_op jit(solution)/shard_map/pallas_call | solution.py:222
  249.6 1.9 slice_bitcast_fusion.13
  251.5 3.0 collective-permute-start.12
  254.5 11.8 %collective-permute-done.19 = bf16[16,16,1152]{2,1,0:T(8,128)(2,1)} collective-permute-done((bf16[16,16,1152]{2,1,0:T(8,128)(2,1)}, bf16[16,16,1152]{2,1,0:T(8,128)(2,1)}, u32[]{:S(2)}, u32[]{:S(2)}) %collective-permute-start.19) | collective-permute-done | bytes 589856 | tf_op jit(solution)/shard_map/ppermute | solution.py:139
  266.3 1.8 pad_maximum_fusion.2
  268.1 1.4 gather_fusion.6
  270.2 28.0 %collective-permute-start.22 = (bf16[16,16,1152]{2,1,0:T(8,128)(2,1)S(1)}, bf16[16,16,1152]{2,1,0:T(8,128)(2,1)}, u32[]{:S(2)}, u32[]{:S(2)}) collective-permute-start(bf16[16,16,1152]{2,1,0:T(8,128)(2,1)S(1)} %gather_fusion.8), channel_id=1, source_target_pairs={{0,8},{4,12},{8,0},{12,4},{1,9},{5,13},{9,1},{13,5},{2,10},{6,14},... | collective-permute-start | bytes 1769480 | tf_op jit(solution)/shard_map/ppermute | solution.py:139
  298.3 1.5 gather_fusion.10
  299.7 1.5 collective-permute-start.23
  301.9 1.8 collective-permute-start.24
  303.9 1.3 fusion.13
  305.2 3.5 collective-permute-done.21.refs_1_
  308.6 2.2 collective-permute-start.13
  310.8 37.8 %collective-permute-done.22.refs_2_ = bf16[16,16,1152]{2,1,0:T(8,128)(2,1)} collective-permute-done((bf16[16,16,1152]{2,1,0:T(8,128)(2,1)S(1)}, bf16[16,16,1152]{2,1,0:T(8,128)(2,1)}, u32[]{:S(2)}, u32[]{:S(2)}) %collective-permute-start.22) | collective-permute-done | bytes 589856 | tf_op jit(solution)/shard_map/ppermute | solution.py:139
  348.6 2.5 collective-permute-start.25
  351.1 0.9 convolution_convert_fusion
  352.5 1.3 collective-permute-start.30
  354.1 1.2 fusion.12
  356.3 0.9 collective-permute-start.27
  357.1 10.0 %collective-permute-done.29.refs_9_ = bf16[16,16,1152]{2,1,0:T(8,128)(2,1)S(1)} collective-permute-done((bf16[16,16,1152]{2,1,0:T(8,128)(2,1)}, bf16[16,16,1152]{2,1,0:T(8,128)(2,1)S(1)}, u32[]{:S(2)}, u32[]{:S(2)}) %collective-permute-start.29) | collective-permute-done | bytes 589856 | tf_op jit(solution)/shard_map/ppermute | solution.py:134
  367.1 1.3 collective-permute-start.32
  368.5 11.3 %collective-permute-done.30.refs_10_ = bf16[16,16,1152]{2,1,0:T(8,128)(2,1)S(1)} collective-permute-done((bf16[16,16,1152]{2,1,0:T(8,128)(2,1)}, bf16[16,16,1152]{2,1,0:T(8,128)(2,1)S(1)}, u32[]{:S(2)}, u32[]{:S(2)}) %collective-permute-start.30) | collective-permute-done | bytes 589856 | tf_op jit(solution)/shard_map/ppermute | solution.py:134
  379.8 1.3 collective-permute-start.33
  381.9 10.5 %collective-permute-done.31.refs_11_ = bf16[16,16,1152]{2,1,0:T(8,128)(2,1)S(1)} collective-permute-done((bf16[16,16,1152]{2,1,0:T(8,128)(2,1)}, bf16[16,16,1152]{2,1,0:T(8,128)(2,1)S(1)}, u32[]{:S(2)}, u32[]{:S(2)}) %collective-permute-start.31) | collective-permute-done | bytes 589856 | tf_op jit(solution)/shard_map/ppermute | solution.py:134
  392.4 0.9 collective-permute-start.34
  393.4 1.2 fusion.11
  395.2 1.3 collective-permute-start.16
  398.5 1.7 copy.89
  400.1 1.7 copy.92
  402.8 15.8 %shard_map.105 = (bf16[16,256,768]{2,1,0:T(8,128)(2,1)}, bf16[16,384,256]{2,1,0:T(8,128)(2,1)}) custom-call(bf16[4,16,64,256]{3,2,1,0:T(8,128)(2,1)} %bitcast.204, bf16[4,16,64,256]{3,2,1,0:T(8,128)(2,1)} %bitcast.205, bf16[16,16,1152]{2,1,0:T(8,128)(2,1)} %copy-done.3, bf16[16,16,1152]{2,1,0:T(8,128)(2,1)} %collective-permute-done.21.refs_1_, ...), custom_call_target="tpu_custom_call" | custom-call | tf_op jit(solution)/shard_map/pallas_call | solution.py:249
  419.5 0.9 copy.96
  420.6 0.9 copy.97
  (146 shorter events, 18.7 us)
Async XLA Ops:
  0.6 4.8 %copy-start.20 = (s32[128,8]{0,1:T(8,128)S(1)}, s32[128,8]{0,1:T(8,128)}, u32[]{:S(2)}) copy-start(s32[128,8]{0,1:T(8,128)} %param.8) | copy-start | bytes 12292
  0.6 5.0 %copy-start.21 = (f32[128,8]{0,1:T(8,128)S(1)}, f32[128,8]{0,1:T(8,128)}, u32[]{:S(2)}) copy-start(f32[128,8]{0,1:T(8,128)} %param.9) | copy-start | bytes 12292
  1.8 35.3 %copy-start.23 = (s32[64]{0:T(128)S(1)}, s32[64]{0:T(128)}, u32[]{:S(2)}) copy-start(s32[64]{0:T(128)} %param.12) | copy-start | bytes 772
  3.1 6.1 %collective-permute-start.2 = (bf16[2,128,256]{2,1,0:T(8,128)(2,1)S(1)}, bf16[2,128,256]{2,1,0:T(8,128)(2,1)S(1)}, u32[]{:S(2)}, u32[]{:S(2)}) collective-permute-start(bf16[2,128,256]{2,1,0:T(8,128)(2,1)S(1)} %get-tuple-element.52), channel_id=1, source_target_pairs={{0,3},{1,2},{2,1},{3,0},{4,7},{5,6},{6,5},{7,4},{8,11},{9,10},{10,... | collective-permute-start | bytes 393224 | tf_op jit(solution)/shard_map/ppermute | solution.py:134
  5.0 7.1 %collective-permute-start.1 = (bf16[2,128,256]{2,1,0:T(8,128)(2,1)S(1)}, bf16[2,128,256]{2,1,0:T(8,128)(2,1)S(1)}, u32[]{:S(2)}, u32[]{:S(2)}) collective-permute-start(bf16[2,128,256]{2,1,0:T(8,128)(2,1)S(1)} %get-tuple-element.53), channel_id=1, source_target_pairs={{0,2},{1,3},{2,0},{3,1},{4,6},{5,7},{6,4},{7,5},{8,10},{9,11},{10,... | collective-permute-start | bytes 393224 | tf_op jit(solution)/shard_map/ppermute | solution.py:134
  5.2 6.8 %collective-permute-start = (bf16[2,128,256]{2,1,0:T(8,128)(2,1)S(1)}, bf16[2,128,256]{2,1,0:T(8,128)(2,1)S(1)}, u32[]{:S(2)}, u32[]{:S(2)}) collective-permute-start(bf16[2,128,256]{2,1,0:T(8,128)(2,1)S(1)} %get-tuple-element.54), channel_id=1, source_target_pairs={{0,1},{1,0},{2,3},{3,2},{4,5},{5,4},{6,7},{7,6},{8,9},{9,8},{10,11... | collective-permute-start | bytes 393224 | tf_op jit(solution)/shard_map/ppermute | solution.py:134
  12.1 25.1 %collective-permute-start.3 = (bf16[4,2,128,256]{3,2,0,1:T(8,128)(2,1)S(1)}, bf16[4,2,128,256]{3,2,0,1:T(8,128)(2,1)S(1)}, u32[]{:S(2)}, u32[]{:S(2)}) collective-permute-start(bf16[4,2,128,256]{3,2,0,1:T(8,128)(2,1)S(1)} %get-tuple-element.50), channel_id=1, source_target_pairs={{0,4},{4,8},{8,12},{12,0},{1,5},{5,9},{9,13},{13,1},{2,6},{6,10},{... | collective-permute-start | bytes 1572872 | tf_op jit(solution)/shard_map/ppermute | solution.py:139
  37.2 15.9 %collective-permute-start.4 = (bf16[4,2,128,256]{3,2,0,1:T(8,128)(2,1)S(1)}, bf16[4,2,128,256]{3,2,0,1:T(8,128)(2,1)S(1)}, u32[]{:S(2)}, u32[]{:S(2)}) collective-permute-start(bf16[4,2,128,256]{3,2,0,1:T(8,128)(2,1)S(1)} %collective-permute-done.3), channel_id=1, source_target_pairs={{0,4},{4,8},{8,12},{12,0},{1,5},{5,9},{9,13},{13,1},{2,6},{6,10},{... | collective-permute-start | bytes 1572872 | tf_op jit(solution)/shard_map/ppermute | solution.py:139
  53.2 14.3 %collective-permute-start.5 = (bf16[4,2,128,256]{3,2,0,1:T(8,128)(2,1)S(1)}, bf16[4,2,128,256]{3,2,0,1:T(8,128)(2,1)S(1)}, u32[]{:S(2)}, u32[]{:S(2)}) collective-permute-start(bf16[4,2,128,256]{3,2,0,1:T(8,128)(2,1)S(1)} %collective-permute-done.4), channel_id=1, source_target_pairs={{0,4},{4,8},{8,12},{12,0},{1,5},{5,9},{9,13},{13,1},{2,6},{6,10},{... | collective-permute-start | bytes 1572872 | tf_op jit(solution)/shard_map/ppermute | solution.py:139
  67.7 2.3 copy-start.4
  89.8 6.3 %collective-permute-start.7 = (bf16[16,64,1152]{2,1,0:T(8,128)(2,1)}, bf16[16,64,1152]{2,1,0:T(8,128)(2,1)S(1)}, u32[]{:S(2)}, u32[]{:S(2)}) collective-permute-start(bf16[16,64,1152]{2,1,0:T(8,128)(2,1)} %get-tuple-element.15), channel_id=1, source_target_pairs={{0,1},{1,0},{2,3},{3,2},{4,5},{5,4},{6,7},{7,6},{8,9},{9,8},{10,11... | collective-permute-start | bytes 7077896 | tf_op jit(solution)/shard_map/ppermute | solution.py:134
  91.7 7.9 %collective-permute-start.6 = (bf16[16,64,1152]{2,1,0:T(8,128)(2,1)}, bf16[16,64,1152]{2,1,0:T(8,128)(2,1)S(1)}, u32[]{:S(2)}, u32[]{:S(2)}) collective-permute-start(bf16[16,64,1152]{2,1,0:T(8,128)(2,1)} %get-tuple-element.13), channel_id=1, source_target_pairs={{0,1},{1,0},{2,3},{3,2},{4,5},{5,4},{6,7},{7,6},{8,9},{9,8},{10,11... | collective-permute-start | bytes 7077896 | tf_op jit(solution)/shard_map/ppermute | solution.py:134
  96.1 55.7 %slice-start = ((s8[4718592]{0:T(1024)(128)(4,1)}), s8[4194304]{0:T(1024)(128)(4,1)S(1)}, s32[]{:S(2)}) async-start(s8[4718592]{0:T(1024)(128)(4,1)} %bitcast.211), calls=%async_computation | async-start | bytes 8388608
  96.1 55.7 %slice-start.1 = ((s8[4718592]{0:T(1024)(128)(4,1)}), s8[524288]{0:T(1024)(128)(4,1)S(1)}, s32[]{:S(2)}) async-start(s8[4718592]{0:T(1024)(128)(4,1)} %bitcast.211), calls=%async_computation.1 | async-start | bytes 1048576
  99.3 52.5 %collective-permute-start.8 = (bf16[16,64,1152]{2,1,0:T(8,128)(2,1)S(1)}, bf16[16,64,1152]{2,1,0:T(8,128)(2,1)S(1)}, u32[]{:S(2)}, u32[]{:S(2)}) collective-permute-start(bf16[16,64,1152]{2,1,0:T(8,128)(2,1)S(1)} %add_convert_fusion), channel_id=1, source_target_pairs={{0,2},{1,3},{2,0},{3,1},{4,6},{5,7},{6,4},{7,5},{8,10},{9,11},{10,... | collective-permute-start | bytes 7077896 | tf_op jit(solution)/shard_map/ppermute | solution.py:134
  153.5 0.9 copy-start.1
  153.5 1.1 copy-start.2
  154.7 57.4 %copy-start = (bf16[16,64,1152]{2,1,0:T(8,128)(2,1)}, bf16[16,64,1152]{2,1,0:T(8,128)(2,1)S(1)}, u32[]{:S(2)}) copy-start(bf16[16,64,1152]{2,1,0:T(8,128)(2,1)S(1)} %pad_maximum_fusion.refs_0_) | copy-start | bytes 7077892
  154.7 51.7 %collective-permute-start.10 = (bf16[16,64,1152]{2,1,0:T(8,128)(2,1)S(1)}, bf16[16,64,1152]{2,1,0:T(8,128)(2,1)}, u32[]{:S(2)}, u32[]{:S(2)}) collective-permute-start(bf16[16,64,1152]{2,1,0:T(8,128)(2,1)S(1)} %pad_maximum_fusion.refs_0_), channel_id=1, source_target_pairs={{0,2},{1,3},{2,0},{3,1},{4,6},{5,7},{6,4},{7,5},{8,10},{9,11},{10,... | collective-permute-start | bytes 7077896 | tf_op jit(solution)/shard_map/ppermute | solution.py:134
  156.5 66.2 %collective-permute-start.9 = (bf16[16,64,1152]{2,1,0:T(8,128)(2,1)S(1)}, bf16[16,64,1152]{2,1,0:T(8,128)(2,1)}, u32[]{:S(2)}, u32[]{:S(2)}) collective-permute-start(bf16[16,64,1152]{2,1,0:T(8,128)(2,1)S(1)} %pad_maximum_fusion.refs_0_), channel_id=1, source_target_pairs={{0,1},{1,0},{2,3},{3,2},{4,5},{5,4},{6,7},{7,6},{8,9},{9,8},{10,11... | collective-permute-start | bytes 7077896 | tf_op jit(solution)/shard_map/ppermute | solution.py:134
  206.3 16.3 %collective-permute-start.11 = (bf16[16,64,1152]{2,1,0:T(8,128)(2,1)}, bf16[16,64,1152]{2,1,0:T(8,128)(2,1)}, u32[]{:S(2)}, u32[]{:S(2)}) collective-permute-start(bf16[16,64,1152]{2,1,0:T(8,128)(2,1)} %collective-permute-done.10.refs_2_), channel_id=1, source_target_pairs={{0,1},{1,0},{2,3},{3,2},{4,5},{5,4},{6,7},{7,6},{8,9},{9,8},{10,11... | collective-permute-start | bytes 7077896 | tf_op jit(solution)/shard_map/ppermute | solution.py:134
  213.3 41.2 %collective-permute-start.20 = (bf16[16,16,1152]{2,1,0:T(8,128)(2,1)}, bf16[16,16,1152]{2,1,0:T(8,128)(2,1)}, u32[]{:S(2)}, u32[]{:S(2)}) collective-permute-start(bf16[16,16,1152]{2,1,0:T(8,128)(2,1)} %get-tuple-element.41), channel_id=1, source_target_pairs={{0,4},{4,8},{8,12},{12,0},{1,5},{5,9},{9,13},{13,1},{2,6},{6,10},{... | collective-permute-start | bytes 1769480 | tf_op jit(solution)/shard_map/ppermute | solution.py:139
  217.3 49.0 %collective-permute-start.19 = (bf16[16,16,1152]{2,1,0:T(8,128)(2,1)}, bf16[16,16,1152]{2,1,0:T(8,128)(2,1)}, u32[]{:S(2)}, u32[]{:S(2)}) collective-permute-start(bf16[16,16,1152]{2,1,0:T(8,128)(2,1)} %get-tuple-element.42), channel_id=1, source_target_pairs={{0,8},{4,12},{8,0},{12,4},{1,9},{5,13},{9,1},{13,5},{2,10},{6,14},... | collective-permute-start | bytes 1769480 | tf_op jit(solution)/shard_map/ppermute | solution.py:139
  217.3 49.0 %collective-permute-start.18 = (bf16[16,16,1152]{2,1,0:T(8,128)(2,1)S(1)}, bf16[16,16,1152]{2,1,0:T(8,128)(2,1)}, u32[]{:S(2)}, u32[]{:S(2)}) collective-permute-start(bf16[16,16,1152]{2,1,0:T(8,128)(2,1)S(1)} %get-tuple-element.40), channel_id=1, source_target_pairs={{0,12},{4,0},{8,4},{12,8},{1,13},{5,1},{9,5},{13,9},{2,14},{6,2},{... | collective-permute-start | bytes 1769480 | tf_op jit(solution)/shard_map/ppermute | solution.py:139
  251.5 52.2 %collective-permute-start.12 = (bf16[4,2,128,256]{3,2,1,0:T(8,128)(2,1)}, bf16[4,2,128,256]{3,2,1,0:T(8,128)(2,1)}, u32[]{:S(2)}, u32[]{:S(2)}) collective-permute-start(bf16[4,2,128,256]{3,2,1,0:T(8,128)(2,1)} %slice_bitcast_fusion.13), channel_id=1, source_target_pairs={{0,4},{4,8},{8,12},{12,0},{1,5},{5,9},{9,13},{13,1},{2,6},{6,10},{... | collective-permute-start | bytes 1572872 | tf_op jit(solution)/shard_map/ppermute | solution.py:139
  268.1 30.1 %copy-start.22 = (s32[16]{0:T(128)S(1)}, s32[16]{0:T(128)}, u32[]{:S(2)}) copy-start(s32[16]{0:T(128)} %gather_fusion.9) | copy-start | bytes 196
  269.5 39.1 %collective-permute-start.21 = (bf16[16,16,1152]{2,1,0:T(8,128)(2,1)}, bf16[16,16,1152]{2,1,0:T(8,128)(2,1)}, u32[]{:S(2)}, u32[]{:S(2)}) collective-permute-start(bf16[16,16,1152]{2,1,0:T(8,128)(2,1)} %gather_fusion.6), channel_id=1, source_target_pairs={{0,4},{4,8},{8,12},{12,0},{1,5},{5,9},{9,13},{13,1},{2,6},{6,10},{... | collective-permute-start | bytes 1769480 | tf_op jit(solution)/shard_map/ppermute | solution.py:139
  270.2 78.4 %collective-permute-start.22 = (bf16[16,16,1152]{2,1,0:T(8,128)(2,1)S(1)}, bf16[16,16,1152]{2,1,0:T(8,128)(2,1)}, u32[]{:S(2)}, u32[]{:S(2)}) collective-permute-start(bf16[16,16,1152]{2,1,0:T(8,128)(2,1)S(1)} %gather_fusion.8), channel_id=1, source_target_pairs={{0,8},{4,12},{8,0},{12,4},{1,9},{5,13},{9,1},{13,5},{2,10},{6,14},... | collective-permute-start | bytes 1769480 | tf_op jit(solution)/shard_map/ppermute | solution.py:139
  299.7 52.3 %collective-permute-start.23 = (bf16[16,16,1152]{2,1,0:T(8,128)(2,1)}, bf16[16,16,1152]{2,1,0:T(8,128)(2,1)}, u32[]{:S(2)}, u32[]{:S(2)}) collective-permute-start(bf16[16,16,1152]{2,1,0:T(8,128)(2,1)} %gather_fusion.10), channel_id=1, source_target_pairs={{0,12},{4,0},{8,4},{12,8},{1,13},{5,1},{9,5},{13,9},{2,14},{6,2},{... | collective-permute-start | bytes 1769480 | tf_op jit(solution)/shard_map/ppermute | solution.py:139
  301.8 80.0 %copy-start.3 = (bf16[16,16,1152]{2,1,0:T(8,128)(2,1)}, bf16[16,16,1152]{2,1,0:T(8,128)(2,1)S(1)}, u32[]{:S(2)}) copy-start(bf16[16,16,1152]{2,1,0:T(8,128)(2,1)S(1)} %gather_fusion.4) | copy-start | bytes 1769476
  301.8 53.5 %copy-start.18 = (f32[4,4,16,128]{3,2,1,0:T(8,128)S(1)}, f32[4,4,16,128]{3,2,1,0:T(8,128)}, u32[]{:S(2)}) copy-start(f32[4,4,16,128]{3,2,1,0:T(8,128)} %get-tuple-element.32) | copy-start | bytes 393220
  301.9 53.5 %copy-start.19 = (pred[4,4,16,128]{3,2,1,0:T(8,128)(4,1)S(1)}, pred[4,4,16,128]{3,2,1,0:T(8,128)(4,1)}, u32[]{:S(2)}) copy-start(pred[4,4,16,128]{3,2,1,0:T(8,128)(4,1)} %get-tuple-element.34) | copy-start | bytes 98308
  301.9 79.2 %copy-start.5 = (bf16[4,4,2,128,256]{4,3,0,1,2:T(8,128)(2,1)S(1)}, bf16[4,4,2,128,256]{4,3,0,1,2:T(8,128)(2,1)}, u32[]{:S(2)}) copy-start(bf16[4,4,2,128,256]{4,3,0,1,2:T(8,128)(2,1)} %copy-done.4) | copy-start | bytes 6291460
  301.9 50.4 %collective-permute-start.24 = (bf16[16,16,1152]{2,1,0:T(8,128)(2,1)S(1)}, bf16[16,16,1152]{2,1,0:T(8,128)(2,1)S(1)}, u32[]{:S(2)}, u32[]{:S(2)}) collective-permute-start(bf16[16,16,1152]{2,1,0:T(8,128)(2,1)S(1)} %gather_fusion.4), channel_id=1, source_target_pairs={{0,1},{1,0},{2,3},{3,2},{4,5},{5,4},{6,7},{7,6},{8,9},{9,8},{10,11... | collective-permute-start | bytes 1769480 | tf_op jit(solution)/shard_map/ppermute | solution.py:134
  303.7 48.9 %collective-permute-start.28 = (bf16[16,16,1152]{2,1,0:T(8,128)(2,1)S(1)}, bf16[16,16,1152]{2,1,0:T(8,128)(2,1)S(1)}, u32[]{:S(2)}, u32[]{:S(2)}) collective-permute-start(bf16[16,16,1152]{2,1,0:T(8,128)(2,1)S(1)} %gather_fusion.4), channel_id=1, source_target_pairs={{0,2},{1,3},{2,0},{3,1},{4,6},{5,7},{6,4},{7,5},{8,10},{9,11},{10,... | collective-permute-start | bytes 1769480 | tf_op jit(solution)/shard_map/ppermute | solution.py:134
  308.6 45.2 %collective-permute-start.13 = (bf16[4,2,128,256]{3,2,1,0:T(8,128)(2,1)S(1)}, bf16[4,2,128,256]{3,2,1,0:T(8,128)(2,1)S(1)}, u32[]{:S(2)}, u32[]{:S(2)}) collective-permute-start(bf16[4,2,128,256]{3,2,1,0:T(8,128)(2,1)S(1)} %fusion.13), channel_id=1, source_target_pairs={{0,4},{4,8},{8,12},{12,0},{1,5},{5,9},{9,13},{13,1},{2,6},{6,10},{... | collective-permute-start | bytes 1572872 | tf_op jit(solution)/shard_map/ppermute | solution.py:139
  348.6 6.7 %collective-permute-start.25 = (bf16[16,16,1152]{2,1,0:T(8,128)(2,1)}, bf16[16,16,1152]{2,1,0:T(8,128)(2,1)S(1)}, u32[]{:S(2)}, u32[]{:S(2)}) collective-permute-start(bf16[16,16,1152]{2,1,0:T(8,128)(2,1)} %collective-permute-done.21.refs_1_), channel_id=1, source_target_pairs={{0,1},{1,0},{2,3},{3,2},{4,5},{5,4},{6,7},{7,6},{8,9},{9,8},{10,11... | collective-permute-start | bytes 1769480 | tf_op jit(solution)/shard_map/ppermute | solution.py:134
  352.0 15.2 %collective-permute-start.29 = (bf16[16,16,1152]{2,1,0:T(8,128)(2,1)}, bf16[16,16,1152]{2,1,0:T(8,128)(2,1)S(1)}, u32[]{:S(2)}, u32[]{:S(2)}) collective-permute-start(bf16[16,16,1152]{2,1,0:T(8,128)(2,1)} %collective-permute-done.21.refs_1_), channel_id=1, source_target_pairs={{0,2},{1,3},{2,0},{3,1},{4,6},{5,7},{6,4},{7,5},{8,10},{9,11},{10,... | collective-permute-start | bytes 1769480 | tf_op jit(solution)/shard_map/ppermute | solution.py:134
  352.3 29.6 %copy-start.6 = (bf16[16,16,1152]{2,1,0:T(8,128)(2,1)}, bf16[16,16,1152]{2,1,0:T(8,128)(2,1)S(1)}, u32[]{:S(2)}) copy-start(bf16[16,16,1152]{2,1,0:T(8,128)(2,1)S(1)} %collective-permute-done.24.refs_4_) | copy-start | bytes 1769476
  352.3 4.0 collective-permute-start.26
  352.5 29.3 %copy-start.7 = (bf16[16,16,1152]{2,1,0:T(8,128)(2,1)}, bf16[16,16,1152]{2,1,0:T(8,128)(2,1)S(1)}, u32[]{:S(2)}) copy-start(bf16[16,16,1152]{2,1,0:T(8,128)(2,1)S(1)} %collective-permute-done.28.refs_8_) | copy-start | bytes 1769476
  352.5 27.2 %collective-permute-start.30 = (bf16[16,16,1152]{2,1,0:T(8,128)(2,1)}, bf16[16,16,1152]{2,1,0:T(8,128)(2,1)S(1)}, u32[]{:S(2)}, u32[]{:S(2)}) collective-permute-start(bf16[16,16,1152]{2,1,0:T(8,128)(2,1)} %collective-permute-done.22.refs_2_), channel_id=1, source_target_pairs={{0,2},{1,3},{2,0},{3,1},{4,6},{5,7},{6,4},{7,5},{8,10},{9,11},{10,... | collective-permute-start | bytes 1769480 | tf_op jit(solution)/shard_map/ppermute | solution.py:134
  353.8 38.6 %collective-permute-start.31 = (bf16[16,16,1152]{2,1,0:T(8,128)(2,1)}, bf16[16,16,1152]{2,1,0:T(8,128)(2,1)S(1)}, u32[]{:S(2)}, u32[]{:S(2)}) collective-permute-start(bf16[16,16,1152]{2,1,0:T(8,128)(2,1)} %collective-permute-done.23.refs_3_), channel_id=1, source_target_pairs={{0,2},{1,3},{2,0},{3,1},{4,6},{5,7},{6,4},{7,5},{8,10},{9,11},{10,... | collective-permute-start | bytes 1769480 | tf_op jit(solution)/shard_map/ppermute | solution.py:134
  355.3 26.5 %copy-start.8 = (bf16[16,16,1152]{2,1,0:T(8,128)(2,1)}, bf16[16,16,1152]{2,1,0:T(8,128)(2,1)S(1)}, u32[]{:S(2)}) copy-start(bf16[16,16,1152]{2,1,0:T(8,128)(2,1)S(1)} %collective-permute-done.25.refs_5_) | copy-start | bytes 1769476
  355.3 38.0 %collective-permute-start.14 = (bf16[4,2,128,256]{3,2,1,0:T(8,128)(2,1)S(1)}, bf16[4,2,128,256]{3,2,1,0:T(8,128)(2,1)S(1)}, u32[]{:S(2)}, u32[]{:S(2)}) collective-permute-start(bf16[4,2,128,256]{3,2,1,0:T(8,128)(2,1)S(1)} %fusion.12), channel_id=1, source_target_pairs={{0,4},{4,8},{8,12},{12,0},{1,5},{5,9},{9,13},{13,1},{2,6},{6,10},{... | collective-permute-start | bytes 1572872 | tf_op jit(solution)/shard_map/ppermute | solution.py:139
  356.2 25.6 %copy-start.10 = (bf16[16,16,1152]{2,1,0:T(8,128)(2,1)}, bf16[16,16,1152]{2,1,0:T(8,128)(2,1)S(1)}, u32[]{:S(2)}) copy-start(bf16[16,16,1152]{2,1,0:T(8,128)(2,1)S(1)} %collective-permute-done.26.refs_6_) | copy-start | bytes 1769476
  356.3 38.4 %collective-permute-start.27 = (bf16[16,16,1152]{2,1,0:T(8,128)(2,1)}, bf16[16,16,1152]{2,1,0:T(8,128)(2,1)S(1)}, u32[]{:S(2)}, u32[]{:S(2)}) collective-permute-start(bf16[16,16,1152]{2,1,0:T(8,128)(2,1)} %collective-permute-done.23.refs_3_), channel_id=1, source_target_pairs={{0,1},{1,0},{2,3},{3,2},{4,5},{5,4},{6,7},{7,6},{8,9},{9,8},{10,11... | collective-permute-start | bytes 1769480 | tf_op jit(solution)/shard_map/ppermute | solution.py:134
  367.1 14.7 %copy-start.9 = (bf16[16,16,1152]{2,1,0:T(8,128)(2,1)}, bf16[16,16,1152]{2,1,0:T(8,128)(2,1)S(1)}, u32[]{:S(2)}) copy-start(bf16[16,16,1152]{2,1,0:T(8,128)(2,1)S(1)} %collective-permute-done.29.refs_9_) | copy-start | bytes 1769476
  367.1 28.1 %collective-permute-start.32 = (bf16[16,16,1152]{2,1,0:T(8,128)(2,1)S(1)}, bf16[16,16,1152]{2,1,0:T(8,128)(2,1)S(1)}, u32[]{:S(2)}, u32[]{:S(2)}) collective-permute-start(bf16[16,16,1152]{2,1,0:T(8,128)(2,1)S(1)} %collective-permute-done.28.refs_8_), channel_id=1, source_target_pairs={{0,1},{1,0},{2,3},{3,2},{4,5},{5,4},{6,7},{7,6},{8,9},{9,8},{10,11... | collective-permute-start | bytes 1769480 | tf_op jit(solution)/shard_map/ppermute | solution.py:134
  379.8 12.6 %copy-start.11 = (bf16[16,16,1152]{2,1,0:T(8,128)(2,1)}, bf16[16,16,1152]{2,1,0:T(8,128)(2,1)S(1)}, u32[]{:S(2)}) copy-start(bf16[16,16,1152]{2,1,0:T(8,128)(2,1)S(1)} %collective-permute-done.30.refs_10_) | copy-start | bytes 1769476
  379.8 16.7 %collective-permute-start.33 = (bf16[16,16,1152]{2,1,0:T(8,128)(2,1)S(1)}, bf16[16,16,1152]{2,1,0:T(8,128)(2,1)S(1)}, u32[]{:S(2)}, u32[]{:S(2)}) collective-permute-start(bf16[16,16,1152]{2,1,0:T(8,128)(2,1)S(1)} %collective-permute-done.29.refs_9_), channel_id=1, source_target_pairs={{0,1},{1,0},{2,3},{3,2},{4,5},{5,4},{6,7},{7,6},{8,9},{9,8},{10,11... | collective-permute-start | bytes 1769480 | tf_op jit(solution)/shard_map/ppermute | solution.py:134
  392.4 6.0 %copy-start.12 = (bf16[16,16,1152]{2,1,0:T(8,128)(2,1)}, bf16[16,16,1152]{2,1,0:T(8,128)(2,1)S(1)}, u32[]{:S(2)}) copy-start(bf16[16,16,1152]{2,1,0:T(8,128)(2,1)S(1)} %collective-permute-done.31.refs_11_) | copy-start | bytes 1769476
  392.4 9.4 %collective-permute-start.34 = (bf16[16,16,1152]{2,1,0:T(8,128)(2,1)S(1)}, bf16[16,16,1152]{2,1,0:T(8,128)(2,1)S(1)}, u32[]{:S(2)}, u32[]{:S(2)}) collective-permute-start(bf16[16,16,1152]{2,1,0:T(8,128)(2,1)S(1)} %collective-permute-done.30.refs_10_), channel_id=1, source_target_pairs={{0,1},{1,0},{2,3},{3,2},{4,5},{5,4},{6,7},{7,6},{8,9},{9,8},{10,11... | collective-permute-start | bytes 1769480 | tf_op jit(solution)/shard_map/ppermute | solution.py:134
  393.3 8.5 %collective-permute-start.35 = (bf16[16,16,1152]{2,1,0:T(8,128)(2,1)S(1)}, bf16[16,16,1152]{2,1,0:T(8,128)(2,1)S(1)}, u32[]{:S(2)}, u32[]{:S(2)}) collective-permute-start(bf16[16,16,1152]{2,1,0:T(8,128)(2,1)S(1)} %collective-permute-done.31.refs_11_), channel_id=1, source_target_pairs={{0,1},{1,0},{2,3},{3,2},{4,5},{5,4},{6,7},{7,6},{8,9},{9,8},{10,11... | collective-permute-start | bytes 1769480 | tf_op jit(solution)/shard_map/ppermute | solution.py:134
  394.6 1.9 copy-start.13
  394.6 24.0 %collective-permute-start.17 = (bf16[2,128,256]{2,1,0:T(8,128)(2,1)S(1)}, bf16[2,128,256]{2,1,0:T(8,128)(2,1)S(1)}, u32[]{:S(2)}, u32[]{:S(2)}) collective-permute-start(bf16[2,128,256]{2,1,0:T(8,128)(2,1)S(1)} %get-tuple-element.46), channel_id=1, source_target_pairs={{0,3},{1,2},{2,1},{3,0},{4,7},{5,6},{6,5},{7,4},{8,11},{9,10},{10,... | collective-permute-start | bytes 393224 | tf_op jit(solution)/shard_map/ppermute | solution.py:134
  395.2 1.3 copy-start.14
  395.2 23.4 %collective-permute-start.16 = (bf16[2,128,256]{2,1,0:T(8,128)(2,1)S(1)}, bf16[2,128,256]{2,1,0:T(8,128)(2,1)S(1)}, u32[]{:S(2)}, u32[]{:S(2)}) collective-permute-start(bf16[2,128,256]{2,1,0:T(8,128)(2,1)S(1)} %get-tuple-element.47), channel_id=1, source_target_pairs={{0,2},{1,3},{2,0},{3,1},{4,6},{5,7},{6,4},{7,5},{8,10},{9,11},{10,... | collective-permute-start | bytes 393224 | tf_op jit(solution)/shard_map/ppermute | solution.py:134
  396.5 0.8 copy-start.15
  397.3 21.3 %collective-permute-start.15 = (bf16[2,128,256]{2,1,0:T(8,128)(2,1)S(1)}, bf16[2,128,256]{2,1,0:T(8,128)(2,1)S(1)}, u32[]{:S(2)}, u32[]{:S(2)}) collective-permute-start(bf16[2,128,256]{2,1,0:T(8,128)(2,1)S(1)} %get-tuple-element.48), channel_id=1, source_target_pairs={{0,1},{1,0},{2,3},{3,2},{4,5},{5,4},{6,7},{7,6},{8,9},{9,8},{10,11... | collective-permute-start | bytes 393224 | tf_op jit(solution)/shard_map/ppermute | solution.py:134
  401.8 0.8 copy-start.16
  401.8 1.0 copy-start.17
